TPU v7x, 32 devices: a whole 2x2x4 slice. The times are simulated.
32 devices in a mesh: grp: 4 (over y, core), row: 8 (over z, x).
Axes of the slice: x: 2, y: 2, z: 4, core: 2. Of those that a mesh axis runs over, the one named last changes fastest.
Arguments:
- landmarks: bfloat16 [1024, 1024], P(('grp', 'row')), may hold values from -6.5 to 6.5
- initial_basis: bfloat16 [1024, 256], P(('grp', 'row')), may hold values from -0.1875 to 0.1875
- points: bfloat16 [32768, 1024], P(('grp', 'row')), may hold values from -6.5 to 6.5
Outputs:
- basis: float32 [1024, 256], P(('grp', 'row'))
- coords: float32 [32768, 256], P(('grp', 'row'))
All inputs are finite; a program needn't handle non-finite values.
Results may differ from a plain program's by a relative error of at most 0.0057.
Values may be sent and summed in bfloat16 or wider, within the bound.
No kernel may reach another device: no remote copies, remote signals or barrier semaphores. Data moves between devices by JAX's collectives and lax.ppermute only.
A program may use at most 128 MiB of HBM per device.

v0:
```python
import math
import jax
import jax.numpy as jnp
from jax import lax
from jax.sharding import PartitionSpec as P

ITERS = 2
spread = 0.25


def squared_rows(rows):
    return jnp.sum(jnp.square(rows.astype(jnp.float32)), axis=1)


def pair_kernel(left, right):
    inner = lax.dot_general(
        left, right, (((1,), (1,)), ((), ())), preferred_element_type=jnp.float32
    )
    dist = squared_rows(left)[:, None] + squared_rows(right)[None, :] - 2.0 * inner
    return jnp.exp(-dist / (spread * left.shape[1]))


def point_terms(anchors, spectral_rows, members, member_sq):
    inner = lax.dot_general(
        anchors, members, (((1,), (1,)), ((), ())), preferred_element_type=jnp.float32
    )
    dist = squared_rows(anchors)[:, None] + member_sq[None, :] - 2.0 * inner
    kernel_part = jnp.exp(-dist / (spread * anchors.shape[1]))
    degree_part = jnp.sum(kernel_part, axis=0)
    numer_part = lax.dot_general(
        kernel_part.astype(jnp.bfloat16),
        spectral_rows,
        (((0,), (0,)), ((), ())),
        preferred_element_type=jnp.float32,
    )
    return (numer_part, degree_part)


def body(landmarks, initial_basis, points):
    local_rows = landmarks.shape[0]
    total = local_rows * lax.axis_size("grp") * lax.axis_size("row")
    row_index = lax.axis_index("row")
    group_rows = lax.all_gather(landmarks, "row", axis=0, tiled=True)
    cross_rows = lax.all_gather(landmarks, "grp", axis=0, tiled=True)
    land_kernel = pair_kernel(group_rows, cross_rows)
    group_degree = lax.psum(jnp.sum(land_kernel, axis=1), "row")
    own_degree = lax.dynamic_slice_in_dim(group_degree, row_index * local_rows, local_rows, 0)
    cross_degree = lax.psum(jnp.sum(land_kernel, axis=0), "grp")
    row_scale = 1.0 / jnp.sqrt(group_degree)
    column_scale = 1.0 / jnp.sqrt(cross_degree)
    affinity = (land_kernel * row_scale[:, None] * column_scale[None, :]).astype(jnp.bfloat16)
    current = initial_basis
    for step in range(ITERS):
        cross_basis = lax.all_gather(current, "grp", axis=0, tiled=True)
        image = lax.psum_scatter(
            jnp.dot(affinity, cross_basis, preferred_element_type=jnp.float32),
            "row",
            scatter_dimension=0,
            tiled=True,
        )
        gram = lax.psum(jnp.dot(image.T, image, precision=lax.Precision.HIGHEST), ("grp", "row"))
        lower = jnp.linalg.cholesky(gram)
        ortho = jax.scipy.linalg.solve_triangular(lower, image.T, lower=True).T
        current = ortho.astype(jnp.bfloat16)
    lam = jnp.diagonal(lower)
    own_scale = 1.0 / jnp.sqrt(own_degree)
    spectral = (ortho * own_scale[:, None] / lam[None, :]).astype(jnp.bfloat16)
    point_sq = squared_rows(points)
    numer_part, degree_part = point_terms(
        lax.all_gather(landmarks, ("grp", "row"), axis=0, tiled=True),
        lax.all_gather(spectral, ("grp", "row"), axis=0, tiled=True),
        points,
        point_sq,
    )
    coords = numer_part / jnp.sqrt(degree_part)[:, None] * math.sqrt(total)
    return (ortho, coords)


def solution(mesh):
    in_specs = (P(("grp", "row"), None), P(("grp", "row"), None), P(("grp", "row"), None))
    out_specs = (P(("grp", "row"), None), P(("grp", "row"), None))
    return jax.shard_map(body, mesh=mesh, in_specs=in_specs, out_specs=out_specs, check_vma=False)
```

profile of v0, /device:TPU:0, one launch (start us, length us, event | category | flops | bytes accessed | tf_op | source)
XLA Modules:
  0.0 683.4 jit_solution(5649184369802876398)
XLA Ops:
  7.2 7.5 %all_gather.19 = bf16[128,1024]{1,0:T(8,128)(2,1)S(1)} all-gather(bf16[32,1024]{1,0:T(8,128)(2,1)} %param.6), channel_id=1, replica_groups=mesh['grp'=4,'row'=8] {'grp'}, dimensions={0}, use_global_device_ids=true | all-gather | bytes 327680 | tf_op jit(solution)/shard_map/all_gather | solution.py:44
  14.7 32.1 %all_gather.18 = bf16[256,1024]{1,0:T(8,128)(2,1)S(1)} all-gather(bf16[32,1024]{1,0:T(8,128)(2,1)} %param.6), channel_id=1, replica_groups=mesh['grp'=4,'row'=8] {'row'}, dimensions={0}, use_global_device_ids=true | all-gather | bytes 589824 | tf_op jit(solution)/shard_map/all_gather | solution.py:43
  46.7 5.4 all_gather.20
  52.9 21.4 %psum.28 = f32[256]{0:T(256)S(1)} all-reduce(f32[256]{0:T(256)S(1)} %get-tuple-element.20), channel_id=1, replica_groups=mesh['grp'=4,'row'=8] {'row'}, use_global_device_ids=true, to_apply=%region_3.0 | all-reduce | flops 256 | bytes 2048 | tf_op jit(solution)/shard_map/psum | solution.py:46
  74.3 5.7 psum.29
  80.9 59.6 %reduce-scatter.3.cloned.1.call-done = f32[32,256]{1,0:T(8,128)} async-done(((f32[256,256]{1,0:T(8,128)}), f32[32,256]{1,0:T(8,128)}) %reduce-scatter.3.cloned.1.call-update) | async-done | bytes 32784 | tf_op jit(solution)/shard_map/reduce_scatter | solution.py:55
  142.6 129.7 %all-reduce.4.cloned.1.call-done = f32[256,256]{0,1:T(8,128)} async-done(((f32[256,256]{0,1:T(8,128)}), f32[256,256]{0,1:T(8,128)}) %all-reduce.4.cloned.1.call-update) | async-done | bytes 262160 | tf_op jit(solution)/shard_map/psum | solution.py:61
  274.4 11.7 %cholesky.130 = f32[128,128]{1,0:T(8,128)S(1)} custom-call(f32[128,128]{1,0:T(8,128)S(1)} %cholesky.194), custom_call_target="Cholesky" | custom-call | tf_op jit(solution)/shard_map/jit(cholesky)/cholesky | solution.py:62
  286.2 9.8 %custom-call.15 = f32[1,128,128]{1,2,0:T(8,128)S(1)} custom-call(f32[1,128,128]{2,1,0:T(8,128)S(1)} %get-tuple-element.53), custom_call_target="InvertDiagBlocksLowerTriangular" | custom-call | tf_op jit(solution)/shard_map/jit(cholesky)/cholesky | solution.py:62
  296.5 11.7 %cholesky.147 = f32[128,128]{1,0:T(8,128)S(1)} custom-call(f32[128,128]{1,0:T(8,128)S(1)} %convolution_subtract_fusion.1), custom_call_target="Cholesky" | custom-call | tf_op jit(solution)/shard_map/jit(cholesky)/cholesky | solution.py:62
  310.4 4.3 while.4
  314.7 19.7 %custom-call.16 = f32[2,128,128]{1,2,0:T(8,128)S(1)} custom-call(f32[2,128,128]{2,1,0:T(8,128)S(1)} %get-tuple-element.18), custom_call_target="InvertDiagBlocksLowerTriangular" | custom-call | tf_op jit(solution)/shard_map/jit(_solve_triangular)/triangular_solve | solution.py:63
  335.0 5.2 all_gather.21
  341.3 61.2 %reduce-scatter.5.cloned.1.call-done = f32[32,256]{1,0:T(8,128)} async-done(((f32[256,256]{1,0:T(8,128)}), f32[32,256]{1,0:T(8,128)}) %reduce-scatter.5.cloned.1.call-update) | async-done | bytes 32784 | tf_op jit(solution)/shard_map/reduce_scatter | solution.py:55
  405.7 128.4 %all-reduce.6.cloned.1.call-done = f32[256,256]{0,1:T(8,128)} async-done(((f32[256,256]{0,1:T(8,128)}), f32[256,256]{0,1:T(8,128)}) %all-reduce.6.cloned.1.call-update) | async-done | bytes 262160 | tf_op jit(solution)/shard_map/psum | solution.py:61
  536.1 11.7 %cholesky.164 = f32[128,128]{1,0:T(8,128)S(1)} custom-call(f32[128,128]{1,0:T(8,128)S(1)} %cholesky.197), custom_call_target="Cholesky" | custom-call | tf_op jit(solution)/shard_map/jit(cholesky)/cholesky | solution.py:62
  547.9 9.8 %custom-call.17 = f32[1,128,128]{1,2,0:T(8,128)S(1)} custom-call(f32[1,128,128]{2,1,0:T(8,128)S(1)} %get-tuple-element.49), custom_call_target="InvertDiagBlocksLowerTriangular" | custom-call | tf_op jit(solution)/shard_map/jit(cholesky)/cholesky | solution.py:62
  558.2 11.7 %cholesky.181 = f32[128,128]{1,0:T(8,128)S(1)} custom-call(f32[128,128]{1,0:T(8,128)S(1)} %convolution_subtract_fusion), custom_call_target="Cholesky" | custom-call | tf_op jit(solution)/shard_map/jit(cholesky)/cholesky | solution.py:62
  572.6 4.2 while.5
  576.8 19.7 %custom-call.18 = f32[2,128,128]{1,2,0:T(8,128)S(1)} custom-call(f32[2,128,128]{2,1,0:T(8,128)S(1)} %get-tuple-element.19), custom_call_target="InvertDiagBlocksLowerTriangular" | custom-call | tf_op jit(solution)/shard_map/jit(_solve_triangular)/triangular_solve | solution.py:63
  596.4 2.3 gather_fusion
  600.0 68.2 %all_gather.23 = bf16[1024,256]{1,0:T(8,128)(2,1)S(1)} all-gather(bf16[32,256]{1,0:T(8,128)(2,1)S(1)} %get-tuple-element.38), channel_id=1, replica_groups=mesh['grp'=4,'row'=8] {'grp','row'}, dimensions={0}, use_global_device_ids=true | all-gather | bytes 540672 | tf_op jit(solution)/shard_map/all_gather | solution.py:71
  670.3 4.3 fusion
  674.6 2.3 divide_multiply_fusion
  (76 shorter events, 27.1 us)
Async XLA Ops:
  7.2 133.4 %reduce-scatter.3.cloned.1.call-start = ((), (), s32[]{:S(2)}) async-start(), calls=%async_computation.2 | async-start | bytes 294912 | tf_op jit(solution)/shard_map/reduce_scatter | solution.py:55
  52.5 352.7 %copy-start = (bf16[1024,1024]{1,0:T(8,128)(2,1)S(1)}, bf16[1024,1024]{1,0:T(8,128)(2,1)}, u32[]{:S(2)}) copy-start(bf16[1024,1024]{1,0:T(8,128)(2,1)} %param.8) | copy-start | bytes 6291460
  80.9 191.5 %all-reduce.4.cloned.1.call-start = ((), (), s32[]{:S(2)}) async-start(), calls=%async_computation.3 | async-start | bytes 524288 | tf_op jit(solution)/shard_map/psum | solution.py:61
  140.6 193.8 %copy-start.2 = (f32[32,256]{1,0:T(8,128)S(1)}, f32[32,256]{1,0:T(8,128)}, u32[]{:S(2)}) copy-start(f32[32,256]{1,0:T(8,128)} %reduce-scatter.3.cloned.1.call-done) | copy-start | bytes 98308
  142.6 259.9 %reduce-scatter.5.cloned.1.call-start = ((), (), s32[]{:S(2)}) async-start(), calls=%async_computation.4 | async-start | bytes 294912 | tf_op jit(solution)/shard_map/reduce_scatter | solution.py:55
  341.2 192.9 %all-reduce.6.cloned.1.call-start = ((), (), s32[]{:S(2)}) async-start(), calls=%async_computation.5 | async-start | bytes 524288 | tf_op jit(solution)/shard_map/psum | solution.py:61
  402.5 196.3 %copy-start.1 = (f32[32,256]{1,0:T(8,128)S(1)}, f32[32,256]{1,0:T(8,128)}, u32[]{:S(2)}) copy-start(f32[32,256]{1,0:T(8,128)} %reduce-scatter.5.cloned.1.call-done) | copy-start | bytes 98308
  404.5 263.7 %all-gather.2.cloned.1.call-start = ((), (), s32[]{:S(2)}) async-start(), calls=%async_computation.6 | async-start | bytes 2162688 | tf_op jit(solution)/shard_map/all_gather | solution.py:70
Sparse Core Ops, SparseCore 0:
  81.0 59.5 reduce-scatter.2
  146.7 125.6 all-reduce.3
  341.3 61.1 reduce-scatter.4
  408.4 125.5 all-reduce.5
  536.9 56.1 all-gather.1
where the time goes:
time: 684 us; the launch traced here: 683 us
  waiting for transfers between devices  380 us (56%)
  blocking collectives  145 us (21%)
  other arithmetic  114 us (17%)
  between operations  16.7 us (2%)
  matrix products  14.9 us (2%)
  local copies, waits for them, and re-layouts  12.7 us (2%)
    psum x2, waiting for transfers between devices, body(): lax.psum(jnp.dot(image.T, image, precision=lax.Precision.HIGHEST), ('grp'...  258 us
    reduce_scatter x2, waiting for transfers between devices, body(): lax.psum_scatter(jnp.dot(affinity, cross_basis, preferred_element_type=jn...  121 us
    another operation x13, other arithmetic, body(): lower = jnp.linalg.cholesky(gram)  68.6 us
    all_gather x1, blocking collectives, body(): lax.all_gather(spectral, ('grp', 'row'), axis=0, tiled=True)  68.2 us
    another operation x5, other arithmetic, body(): ortho = jax.scipy.linalg.solve_triangular(lower, image.T, lower=True).T  39.4 us
    all_gather x1, blocking collectives, body(): group_rows = lax.all_gather(landmarks, 'row', axis=0, tiled=True)  32.1 us
    psum x1, blocking collectives, body(): group_degree = lax.psum(jnp.sum(land_kernel, axis=1), 'row')  21.4 us
  transfers between devices with their start and end apart: 5, of which 4 were waited for; matrix products, arithmetic and copies ran while one was open for 9% of the time, Pallas kernels for 0%

commit v1 on v0

--- a/solution.py
+++ b/solution.py
@@ -58,7 +58,12 @@
             scatter_dimension=0,
             tiled=True,
         )
-        gram = lax.psum(jnp.dot(image.T, image, precision=lax.Precision.HIGHEST), ("grp", "row"))
+        gram = jnp.sum(
+            lax.all_gather(
+                jnp.dot(image.T, image, precision=lax.Precision.HIGHEST), ("grp", "row")
+            ),
+            axis=0,
+        )
         lower = jnp.linalg.cholesky(gram)
         ortho = jax.scipy.linalg.solve_triangular(lower, image.T, lower=True).T
         current = ortho.astype(jnp.bfloat16)

time: 684 us -> 638 us (0.933)
  waiting for transfers between devices: 380 us -> 325 us
    psum x2 -> x0, waiting for transfers between devices: 258 us -> none  [body(): lax.psum(jnp.dot(image.T, image, precision=lax.Precision.HIGHEST), ('grp'...]
    all_gather x0 -> x2, waiting for transfers between devices: none -> 149 us  [body(): lax.all_gather(jnp.dot(image.T, image, precision=lax.Precision.HIGHEST),...]
    all_gather x1, waiting for transfers between devices: 0.01 us -> 55.8 us  [body(): lax.all_gather(landmarks, ('grp', 'row'), axis=0, tiled=True)]
    reduce_sum x0 -> x2, other arithmetic: none -> 7.86 us  [body(): jnp.sum(lax.all_gather(jnp.dot(image.T, image, precision=lax.Precision.HI...]
  transfers between devices with their start and end apart: 5 -> 5, of which waited for: 4 -> 5; matrix products, arithmetic and copies ran while one was open for 9% -> 2% of each run, Pallas kernels for 0% -> 0%
where the time goes in v1:
time: 638 us; the launch traced here: 637 us
  waiting for transfers between devices  325 us (51%)
  blocking collectives  146 us (23%)
  other arithmetic  120 us (19%)
  matrix products  18.8 us (3%)
  between operations  16.7 us (3%)
  local copies, waits for them, and re-layouts  10.8 us (2%)
    all_gather x2, waiting for transfers between devices, body(): lax.all_gather(jnp.dot(image.T, image, precision=lax.Precision.HIGHEST),...  149 us
    reduce_scatter x2, waiting for transfers between devices, body(): lax.psum_scatter(jnp.dot(affinity, cross_basis, preferred_element_type=jn...  120 us
    all_gather x1, blocking collectives, body(): lax.all_gather(spectral, ('grp', 'row'), axis=0, tiled=True)  69 us
    another operation x13, other arithmetic, body(): lower = jnp.linalg.cholesky(gram)  68.8 us
    all_gather x1, waiting for transfers between devices, body(): lax.all_gather(landmarks, ('grp', 'row'), axis=0, tiled=True)  55.8 us
    another operation x5, other arithmetic, body(): ortho = jax.scipy.linalg.solve_triangular(lower, image.T, lower=True).T  39.4 us
    all_gather x1, blocking collectives, body(): group_rows = lax.all_gather(landmarks, 'row', axis=0, tiled=True)  33.3 us
    psum x1, blocking collectives, body(): group_degree = lax.psum(jnp.sum(land_kernel, axis=1), 'row')  21.5 us
  transfers between devices with their start and end apart: 5, of which 5 were waited for; matrix products, arithmetic and copies ran while one was open for 2% of the time, Pallas kernels for 0%

profile of v1, /device:TPU:0, one launch (start us, length us, event | category | flops | bytes accessed | tf_op | source)
XLA Modules:
  0.0 637.4 jit_solution(257580165895405580)
XLA Ops:
  7.2 33.3 %all_gather.30 = bf16[256,1024]{1,0:T(8,128)(2,1)S(1)} all-gather(bf16[32,1024]{1,0:T(8,128)(2,1)} %param.6), channel_id=1, replica_groups=mesh['grp'=4,'row'=8] {'row'}, dimensions={0}, use_global_device_ids=true | all-gather | bytes 589824 | tf_op jit(solution)/shard_map/all_gather | solution.py:43
  40.5 6.0 all_gather.31
  47.2 21.5 %psum.14 = f32[256]{0:T(256)S(1)} all-reduce(f32[256]{0:T(256)S(1)} %get-tuple-element.20), channel_id=1, replica_groups=mesh['grp'=4,'row'=8] {'row'}, use_global_device_ids=true, to_apply=%region_3.0 | all-reduce | flops 256 | bytes 2048 | tf_op jit(solution)/shard_map/psum | solution.py:46
  68.6 5.7 psum.15
  74.3 5.4 all_gather.32
  80.7 59.7 %reduce-scatter.3.cloned.1.call-done = f32[32,256]{1,0:T(8,128)} async-done(((f32[256,256]{1,0:T(8,128)}), f32[32,256]{1,0:T(8,128)}) %reduce-scatter.3.cloned.1.call-update) | async-done | bytes 32784 | tf_op jit(solution)/shard_map/reduce_scatter | solution.py:55
  142.4 77.7 %all-gather.8.cloned.1.call-done = f32[8192,256]{1,0:T(8,128)} async-done(((f32[256,256]{1,0:T(8,128)}), f32[8192,256]{1,0:T(8,128)}) %all-gather.8.cloned.1.call-update) | async-done | bytes 8388624 | tf_op jit(solution)/shard_map/all_gather | solution.py:62
  220.1 3.9 reduce_sum.85
  224.3 11.7 %cholesky.130 = f32[128,128]{1,0:T(8,128)S(1)} custom-call(f32[128,128]{1,0:T(8,128)S(1)} %cholesky.194), custom_call_target="Cholesky" | custom-call | tf_op jit(solution)/shard_map/jit(cholesky)/cholesky | solution.py:67
  236.0 9.8 %custom-call.15 = f32[1,128,128]{1,2,0:T(8,128)S(1)} custom-call(f32[1,128,128]{2,1,0:T(8,128)S(1)} %get-tuple-element.53), custom_call_target="InvertDiagBlocksLowerTriangular" | custom-call | tf_op jit(solution)/shard_map/jit(cholesky)/cholesky | solution.py:67
  246.3 11.7 %cholesky.147 = f32[128,128]{1,0:T(8,128)S(1)} custom-call(f32[128,128]{1,0:T(8,128)S(1)} %convolution_subtract_fusion.1), custom_call_target="Cholesky" | custom-call | tf_op jit(solution)/shard_map/jit(cholesky)/cholesky | solution.py:67
  260.3 4.3 while.4
  264.6 19.7 %custom-call.16 = f32[2,128,128]{1,2,0:T(8,128)S(1)} custom-call(f32[2,128,128]{2,1,0:T(8,128)S(1)} %get-tuple-element.18), custom_call_target="InvertDiagBlocksLowerTriangular" | custom-call | tf_op jit(solution)/shard_map/jit(_solve_triangular)/triangular_solve | solution.py:68
  284.9 5.2 all_gather.35
  291.7 60.2 %reduce-scatter.5.cloned.1.call-done = f32[32,256]{1,0:T(8,128)} async-done(((f32[256,256]{1,0:T(8,128)}), f32[32,256]{1,0:T(8,128)}) %reduce-scatter.5.cloned.1.call-update) | async-done | bytes 32784 | tf_op jit(solution)/shard_map/reduce_scatter | solution.py:55
  354.5 55.8 %all-gather.6.cloned.1.call-done = bf16[1024,1024]{1,0:T(8,128)(2,1)} async-done(((bf16[32,1024]{1,0:T(8,128)(2,1)}), bf16[1024,1024]{1,0:T(8,128)(2,1)}) %all-gather.6.cloned.1.call-update) | async-done | bytes 2097168 | tf_op jit(solution)/shard_map/all_gather | solution.py:75
  412.3 6.2 fusion
  418.5 71.1 %all-gather.10.cloned.1.call-done = f32[8192,256]{1,0:T(8,128)} async-done(((f32[256,256]{1,0:T(8,128)}), f32[8192,256]{1,0:T(8,128)}) %all-gather.10.cloned.1.call-update) | async-done | bytes 8388624 | tf_op jit(solution)/shard_map/all_gather | solution.py:62
  493.7 11.7 %cholesky.164 = f32[128,128]{1,0:T(8,128)S(1)} custom-call(f32[128,128]{1,0:T(8,128)S(1)} %cholesky.197), custom_call_target="Cholesky" | custom-call | tf_op jit(solution)/shard_map/jit(cholesky)/cholesky | solution.py:67
  505.5 9.8 %custom-call.17 = f32[1,128,128]{1,2,0:T(8,128)S(1)} custom-call(f32[1,128,128]{2,1,0:T(8,128)S(1)} %get-tuple-element.49), custom_call_target="InvertDiagBlocksLowerTriangular" | custom-call | tf_op jit(solution)/shard_map/jit(cholesky)/cholesky | solution.py:67
  515.8 11.9 %cholesky.181 = f32[128,128]{1,0:T(8,128)S(1)} custom-call(f32[128,128]{1,0:T(8,128)S(1)} %convolution_subtract_fusion), custom_call_target="Cholesky" | custom-call | tf_op jit(solution)/shard_map/jit(cholesky)/cholesky | solution.py:67
  534.3 19.7 %custom-call.18 = f32[2,128,128]{1,2,0:T(8,128)S(1)} custom-call(f32[2,128,128]{2,1,0:T(8,128)S(1)} %get-tuple-element.19), custom_call_target="InvertDiagBlocksLowerTriangular" | custom-call | tf_op jit(solution)/shard_map/jit(_solve_triangular)/triangular_solve | solution.py:68
  557.5 69.0 %all_gather.39 = bf16[1024,256]{1,0:T(8,128)(2,1)S(1)} all-gather(bf16[32,256]{1,0:T(8,128)(2,1)S(1)} %get-tuple-element.38), channel_id=1, replica_groups=mesh['grp'=4,'row'=8] {'grp','row'}, dimensions={0}, use_global_device_ids=true | all-gather | bytes 540672 | tf_op jit(solution)/shard_map/all_gather | solution.py:76
  626.5 4.4 divide_multiply_fusion
  (78 shorter events, 33.4 us)
Async XLA Ops:
  7.2 133.2 %reduce-scatter.3.cloned.1.call-start = ((), (), s32[]{:S(2)}) async-start(), calls=%async_computation.2 | async-start | bytes 294912 | tf_op jit(solution)/shard_map/reduce_scatter | solution.py:55
  80.7 139.4 %all-gather.8.cloned.1.call-start = ((), (), s32[]{:S(2)}) async-start(), calls=%async_computation.5 | async-start | bytes 8650752 | tf_op jit(solution)/shard_map/all_gather | solution.py:62
  142.4 209.5 %reduce-scatter.5.cloned.1.call-start = ((), (), s32[]{:S(2)}) async-start(), calls=%async_computation.3 | async-start | bytes 294912 | tf_op jit(solution)/shard_map/reduce_scatter | solution.py:55
  220.1 64.1 %copy-start.2 = (f32[32,256]{1,0:T(8,128)S(1)}, f32[32,256]{1,0:T(8,128)}, u32[]{:S(2)}) copy-start(f32[32,256]{1,0:T(8,128)} %reduce-scatter.3.cloned.1.call-done) | copy-start | bytes 98308
  224.1 129.9 %copy-start = (bf16[1024,1024]{1,0:T(8,128)(2,1)S(1)}, bf16[1024,1024]{1,0:T(8,128)(2,1)}, u32[]{:S(2)}) copy-start(bf16[1024,1024]{1,0:T(8,128)(2,1)} %param.8) | copy-start | bytes 6291460
  291.1 119.2 %all-gather.6.cloned.1.call-start = ((), (), s32[]{:S(2)}) async-start(), calls=%async_computation.4 | async-start | bytes 2162688 | tf_op jit(solution)/shard_map/all_gather | solution.py:75
  291.6 198.0 %all-gather.10.cloned.1.call-start = ((), (), s32[]{:S(2)}) async-start(), calls=%async_computation.6 | async-start | bytes 8650752 | tf_op jit(solution)/shard_map/all_gather | solution.py:62
  493.5 60.5 %copy-start.1 = (f32[32,256]{1,0:T(8,128)S(1)}, f32[32,256]{1,0:T(8,128)}, u32[]{:S(2)}) copy-start(f32[32,256]{1,0:T(8,128)} %reduce-scatter.5.cloned.1.call-done) | copy-start | bytes 98308
Sparse Core Ops, SparseCore 0:
  80.8 59.5 reduce-scatter.2
  144.0 76.1 all-gather.7
  291.2 60.6 reduce-scatter.4
  354.7 55.4 all-gather.5
  413.6 75.9 all-gather.9
